TPU v7x, 768 devices: a whole 4x8x12 slice. The times are simulated.
768 devices in a mesh: segment: 12 (over z), ctx: 16 (over x, y_hi, core), tp: 4 (over y_lo).
Axes of the slice: x: 4, y: 8 (y_hi: 2, y_lo: 4; y = y_hi * 4 + y_lo), z: 12, core: 2. Of those that a mesh axis runs over, the one named last changes fastest.
Arguments:
- hidden_in: bfloat16 [12, 2048, 4096], P('segment', 'ctx')
- norm_gain: bfloat16 [12, 4096], P('segment'), may hold values from 0.5 to 1.5
- query_weight: bfloat16 [12, 4096, 4096], P('segment', None, 'tp')
- keyval_weight: bfloat16 [12, 4096, 2048], P('segment', None, 'tp')
- output_weight: bfloat16 [12, 4096, 4096], P('segment', 'tp'), may hold values from -0.1875 to 0.1875
- windows: int32 [12], P('segment'), may hold values from 192 to 384, as said below
Outputs:
- handed: bfloat16 [12, 2048, 4096], P('segment', 'ctx', 'tp')
Inputs may be any that keep to these rules, and one draw needn't show every extreme that they name: `windows`: one section's window is exactly 384 tokens.
All inputs are finite; a program needn't handle non-finite values.
Results may differ from a plain program's by a relative error of at most 0.006.
The roundings to bfloat16 on the way count: a program that leaves them out, or rounds other values in their place, can miss the bound.
Values may be sent and summed in bfloat16 or wider, within the bound.
A program may use at most 128 MiB of HBM per device.

v0:
```python
import jax
import jax.numpy as jnp
from jax import lax
from jax.sharding import PartitionSpec as P

HD = 128
REACH = 3


NORM_EPS = 1e-05


def from_behind(value, axis, steps):
    count = lax.axis_size(axis)
    initial, last = (max(0, -steps), min(count, count - steps))
    return lax.ppermute(value, axis, [(source, source + steps) for source in range(initial, last)])


def passed_along(value, axis, steps):
    count = lax.axis_size(axis)
    pairs = [(source, (source + steps) % count) for source in range(count)]
    return lax.ppermute(value, axis, pairs)


def rotate(vector, positions):
    half_dim = vector.shape[-1] // 2
    inverse = 10000.0 ** (-jnp.arange(half_dim, dtype=jnp.float32) / half_dim)
    angles = positions.astype(jnp.float32)[:, None, None] * inverse[None, None, :]
    cosine = jnp.cos(angles)
    sine = jnp.sin(angles)
    first_half = vector[..., :half_dim]
    second_half = vector[..., half_dim:]
    return jnp.concatenate(
        [first_half * cosine - second_half * sine, second_half * cosine + first_half * sine],
        axis=-1,
    )


def attend(queries, keys, values, query_pos, key_pos, width):
    scores = jnp.einsum("qgd,kd->gqk", queries, keys, preferred_element_type=jnp.float32) * HD ** (
        -0.5
    )
    distance = query_pos[:, None] - key_pos[None, :]
    inside = ((distance >= 0) & (distance < width) & (key_pos[None, :] >= 0))[None]
    scores = jnp.where(inside, scores, jnp.float32(-1e30))
    highest = jnp.max(scores, axis=2, keepdims=True)
    expo = jnp.where(inside, jnp.exp(scores - highest), jnp.float32(0.0))
    probs = (expo / jnp.sum(expo, axis=2, keepdims=True)).astype(jnp.bfloat16)
    return jnp.einsum("gqk,kd->qgd", probs, values, preferred_element_type=jnp.float32).astype(
        jnp.bfloat16
    )


def normalize(token_rows, gain_row):
    wide_rows = token_rows.astype(jnp.float32)
    mean_square = jnp.mean(wide_rows * wide_rows, axis=1, keepdims=True)
    return (
        wide_rows * lax.rsqrt(mean_square + NORM_EPS) * gain_row.astype(jnp.float32)[None, :]
    ).astype(jnp.bfloat16)


def body(hidden_in, norm_gain, query_weight, keyval_weight, output_weight, windows):
    token_rows = hidden_in[0]
    row_count = token_rows.shape[0]
    head_count = query_weight.shape[2] // HD
    kv_count = keyval_weight.shape[2] // (2 * HD)
    group = head_count // kv_count
    normed = normalize(token_rows, norm_gain[0])
    first_row = lax.axis_index("ctx") * row_count
    local_pos = first_row + jnp.arange(row_count, dtype=jnp.int32)
    queries = jnp.dot(normed, query_weight[0], preferred_element_type=jnp.float32).reshape(
        row_count, head_count, HD
    )
    queries = rotate(queries, local_pos).astype(jnp.bfloat16)

    def project(rows_in, positions):
        key_value = jnp.dot(rows_in, keyval_weight[0], preferred_element_type=jnp.float32).reshape(
            rows_in.shape[0], kv_count, 2, HD
        )
        return (
            rotate(key_value[:, :, 0], positions).astype(jnp.bfloat16),
            key_value[:, :, 1].astype(jnp.bfloat16),
        )

    own_keys, own_values = project(normed, local_pos)
    key_list = []
    value_list = []
    for offset in range(REACH, 0, -1):
        earlier = from_behind(normed, "ctx", offset)
        earlier_keys, earlier_values = project(earlier, local_pos - offset * row_count)
        key_list.append(earlier_keys)
        value_list.append(earlier_values)
    all_keys = jnp.concatenate(key_list + [own_keys], axis=0)
    all_values = jnp.concatenate(value_list + [own_values], axis=0)
    key_pos = first_row - REACH * row_count + jnp.arange((REACH + 1) * row_count, dtype=jnp.int32)
    outs_list = []
    for kv_index in range(kv_count):
        outs_list.append(
            attend(
                queries[:, kv_index * group : (kv_index + 1) * group],
                all_keys[:, kv_index],
                all_values[:, kv_index],
                local_pos,
                key_pos,
                windows[0],
            )
        )
    attn = jnp.concatenate(outs_list, axis=1).reshape(row_count, head_count * HD)
    head_term = jnp.dot(attn, output_weight[0], preferred_element_type=jnp.float32)
    summed = lax.psum_scatter(head_term, "tp", scatter_dimension=1, tiled=True).astype(jnp.bfloat16)
    passed = passed_along(summed, "segment", 1)
    return passed[None]


def solution(mesh):
    in_specs = (
        P("segment", "ctx", None),
        P("segment", None),
        P("segment", None, "tp"),
        P("segment", None, "tp"),
        P("segment", "tp", None),
        P("segment"),
    )
    out_specs = P("segment", "ctx", "tp")
    return jax.shard_map(body, mesh=mesh, in_specs=in_specs, out_specs=out_specs, check_vma=False)
```

profile of v0, /device:TPU:56, one launch (start us, length us, event | category | flops | bytes accessed | tf_op | source)
XLA Modules:
  0.0 206.9 jit_solution(5559781424724557173)
XLA Ops:
  6.5 0.0 reduce-scatter.2.cloned.1.call-start
  6.5 1.5 fusion.8
  8.1 0.7 mul.337
  8.8 1.5 fusion.10
  10.4 1.9 collective-permute-start.2
  12.3 5.6 %collective-permute-start.1 = (bf16[128,4096]{1,0:T(8,128)(2,1)S(1)}, bf16[128,4096]{1,0:T(8,128)(2,1)}, u32[]{:S(2)}, u32[]{:S(2)}) collective-permute-start(bf16[128,4096]{1,0:T(8,128)(2,1)S(1)} %fusion.10), channel_id=1, source_target_pairs={{0,8},{4,12},{8,16},{12,20},{16,24},{20,28},{24,32},{28,36},{32,40... | collective-permute-start | bytes 3145736 | tf_op jit(solution)/shard_map/ppermute | solution.py:16
  17.9 9.2 %collective-permute-start = (bf16[128,4096]{1,0:T(8,128)(2,1)S(1)}, bf16[128,4096]{1,0:T(8,128)(2,1)}, u32[]{:S(2)}, u32[]{:S(2)}) collective-permute-start(bf16[128,4096]{1,0:T(8,128)(2,1)S(1)} %fusion.10), channel_id=1, source_target_pairs={{0,12},{4,16},{8,20},{12,24},{16,28},{20,32},{24,36},{28,40},{32,4... | collective-permute-start | bytes 3145736 | tf_op jit(solution)/shard_map/ppermute | solution.py:16
  27.2 6.9 %dot_general.39 = bf16[2,2,128,4096]{2,1,0,3:T(2,128)(2,1)} reshape(bf16[512,4096]{0,1:T(8,128)(2,1)} %bitcast.141) | data formatting | bytes 8388608 | tf_op jit(solution)/shard_map/dot_general | solution.py:77
  34.1 0.0 copy-start.2
  34.1 11.3 %copy.25 = bf16[2,2,128,4096]{3,2,0,1:T(8,128)(2,1)} copy(bf16[2,2,128,4096]{2,1,0,3:T(2,128)(2,1)} %dot_general.39) | data formatting | bytes 8388608 | tf_op jit(solution)/shard_map/dot_general | solution.py:77
  45.4 0.0 copy-done.2
  45.4 3.5 %fusion.25 = f32[128,2,2,128]{0,3,1,2:T(8,128)S(1)} fusion(bf16[2,2,128,4096]{3,2,0,1:T(8,128)(2,1)} %copy.25, bf16[1,128,4096]{2,1,0:T(8,128)(2,1)S(1)} %copy-done.2, f32[4096]{0:T(1024)S(1)} %bitcast.145, f32[128]{0:T(128)S(1)} %add_rsqrt_fusion), kind=kOutput, calls=%fused_computation.31 | convolution fusion | flops 538968064 | bytes 5521920 | tf_op jit(solution)/shard_map/dot_general | solution.py:77
  49.6 11.3 %copy.41 = bf16[1024,4096]{1,0:T(8,128)(2,1)} copy(bf16[1024,4096]{0,1:T(8,128)(2,1)} %bitcast.140) | data formatting | bytes 16777216 | tf_op jit(solution)/shard_map/dot_general | solution.py:71
  60.9 0.5 multiply_cosine_fusion.3
  61.5 0.0 copy-start
  61.5 5.9 %fusion.28 = f32[128,8,128]{0,2,1:T(8,128)S(1)} fusion(bf16[8,128,4096]{2,1,0:T(8,128)(2,1)} %bitcast.139, bf16[1,128,4096]{2,1,0:T(8,128)(2,1)S(1)} %copy-done.2, f32[4096]{0:T(1024)S(1)} %bitcast.146, f32[128]{0:T(128)S(1)} %add_rsqrt_fusion), kind=kOutput, calls=%fused_computation.34 | convolution fusion | flops 1075838976 | bytes 9978368 | tf_op jit(solution)/shard_map/dot_general | solution.py:71
  67.4 0.2 fusion.37
  67.6 0.1 subtract_convert_fusion
  67.7 0.0 collective-permute-done.1
  67.7 0.0 copy-done
  67.7 2.5 %fusion.32 = f32[128,2,2,128]{0,3,1,2:T(8,128)S(1)} fusion(bf16[2,2,128,4096]{3,2,0,1:T(8,128)(2,1)S(1)} %copy-done, bf16[128,4096]{1,0:T(8,128)(2,1)} %collective-permute-done.1), kind=kOutput, calls=%fused_computation.38 | convolution fusion | flops 536870912 | bytes 5505024 | tf_op jit(solution)/shard_map/dot_general | solution.py:77
  70.3 0.0 copy-start.1
  70.3 0.0 collective-permute-done.2
  70.3 1.3 fusion.30
  71.7 31.5 %collective-permute-done = bf16[128,4096]{1,0:T(8,128)(2,1)} collective-permute-done((bf16[128,4096]{1,0:T(8,128)(2,1)S(1)}, bf16[128,4096]{1,0:T(8,128)(2,1)}, u32[]{:S(2)}, u32[]{:S(2)}) %collective-permute-start) | collective-permute-done | bytes 1048608 | tf_op jit(solution)/shard_map/ppermute | solution.py:16
  103.2 0.0 copy-done.1
  103.2 3.0 %fusion.4 = f32[128,2,2,128]{0,3,2,1:T(8,128)S(1)} fusion(bf16[2,2,128,4096]{2,1,0,3:T(2,128)(2,1)S(1)} %copy-done.1, bf16[128,4096]{1,0:T(8,128)(2,1)} %collective-permute-done), kind=kOutput, calls=%fused_computation.4 | convolution fusion | flops 536870912 | bytes 5505024 | tf_op jit(solution)/shard_map/dot_general | solution.py:77
  106.4 0.6 fusion.84
  107.0 0.6 fusion.85
  107.6 0.8 fusion.23
  108.4 0.8 fusion.24
  109.2 6.0 %fusion.2 = f32[128,4096]{1,0:T(8,128)} fusion(bf16[128,1024]{0,1:T(8,128)(2,1)S(1)} %bitcast.142, bf16[1,1024,4096]{2,1,0:T(8,128)(2,1)} %param.10), kind=kOutput, calls=%fused_computation.2 | convolution fusion | flops 1073741824 | bytes 10747904 | tf_op jit(solution)/shard_map/dot_general | solution.py:109
  115.2 0.0 reduce-scatter.2.cloned.1.call-update
  115.3 70.2 %reduce-scatter.2.cloned.1.call-done = f32[128,1024]{1,0:T(8,128)} async-done(((f32[128,4096]{1,0:T(8,128)}), f32[128,1024]{1,0:T(8,128)}) %reduce-scatter.2.cloned.1.call-update) | async-done | bytes 524304 | tf_op jit(solution)/shard_map/reduce_scatter | solution.py:110
  185.4 1.1 convert_element_type.112
  186.5 3.5 %collective-permute-start.3 = (bf16[128,1024]{1,0:T(8,128)(2,1)S(1)}, bf16[128,1024]{1,0:T(8,128)(2,1)S(1)}, u32[]{:S(2)}, u32[]{:S(2)}) collective-permute-start(bf16[128,1024]{1,0:T(8,128)(2,1)S(1)} %convert_element_type.112), channel_id=1, source_target_pairs={{0,64},{64,128},{128,192},{192,256},{256,320},{320,384},{384,448},... | collective-permute-start | bytes 786440 | tf_op jit(solution)/shard_map/ppermute | solution.py:22
  190.0 9.3 %collective-permute-done.3 = bf16[128,1024]{1,0:T(8,128)(2,1)S(1)} collective-permute-done((bf16[128,1024]{1,0:T(8,128)(2,1)S(1)}, bf16[128,1024]{1,0:T(8,128)(2,1)S(1)}, u32[]{:S(2)}, u32[]{:S(2)}) %collective-permute-start.3) | collective-permute-done | bytes 262176 | tf_op jit(solution)/shard_map/ppermute | solution.py:22
  199.3 0.7 copy.47
  (22 shorter events, 0.3 us)
Async XLA Ops:
  6.5 178.9 %reduce-scatter.2.cloned.1.call-start = ((), (), s32[]{:S(2)}) async-start(), calls=%async_computation.1 | async-start | bytes 2621440 | tf_op jit(solution)/shard_map/reduce_scatter | solution.py:110
  10.4 60.0 %collective-permute-start.2 = (bf16[128,4096]{1,0:T(8,128)(2,1)S(1)}, bf16[128,4096]{1,0:T(8,128)(2,1)S(1)}, u32[]{:S(2)}, u32[]{:S(2)}) collective-permute-start(bf16[128,4096]{1,0:T(8,128)(2,1)S(1)} %fusion.10), channel_id=1, source_target_pairs={{0,4},{4,8},{8,12},{12,16},{16,20},{20,24},{24,28},{28,32},{32,36}... | collective-permute-start | bytes 3145736 | tf_op jit(solution)/shard_map/ppermute | solution.py:16
  12.3 55.4 %collective-permute-start.1 = (bf16[128,4096]{1,0:T(8,128)(2,1)S(1)}, bf16[128,4096]{1,0:T(8,128)(2,1)}, u32[]{:S(2)}, u32[]{:S(2)}) collective-permute-start(bf16[128,4096]{1,0:T(8,128)(2,1)S(1)} %fusion.10), channel_id=1, source_target_pairs={{0,8},{4,12},{8,16},{12,20},{16,24},{20,28},{24,32},{28,36},{32,40... | collective-permute-start | bytes 3145736 | tf_op jit(solution)/shard_map/ppermute | solution.py:16
  17.9 85.2 %collective-permute-start = (bf16[128,4096]{1,0:T(8,128)(2,1)S(1)}, bf16[128,4096]{1,0:T(8,128)(2,1)}, u32[]{:S(2)}, u32[]{:S(2)}) collective-permute-start(bf16[128,4096]{1,0:T(8,128)(2,1)S(1)} %fusion.10), channel_id=1, source_target_pairs={{0,12},{4,16},{8,20},{12,24},{16,28},{20,32},{24,36},{28,40},{32,4... | collective-permute-start | bytes 3145736 | tf_op jit(solution)/shard_map/ppermute | solution.py:16
  34.1 11.3 %copy-start.2 = (bf16[1,128,4096]{2,1,0:T(8,128)(2,1)S(1)}, bf16[1,128,4096]{2,1,0:T(8,128)(2,1)}, u32[]{:S(2)}) copy-start(bf16[1,128,4096]{2,1,0:T(8,128)(2,1)} %param.6) | copy-start | bytes 3145732
  61.5 6.2 %copy-start = (bf16[2,2,128,4096]{3,2,0,1:T(8,128)(2,1)S(1)}, bf16[2,2,128,4096]{3,2,0,1:T(8,128)(2,1)}, u32[]{:S(2)}) copy-start(bf16[2,2,128,4096]{3,2,0,1:T(8,128)(2,1)} %copy.25) | copy-start | bytes 12582916
  70.3 32.9 %copy-start.1 = (bf16[2,2,128,4096]{2,1,0,3:T(2,128)(2,1)S(1)}, bf16[2,2,128,4096]{2,1,0,3:T(2,128)(2,1)}, u32[]{:S(2)}) copy-start(bf16[2,2,128,4096]{2,1,0,3:T(2,128)(2,1)} %dot_general.39) | copy-start | bytes 12582916
  186.5 12.8 %collective-permute-start.3 = (bf16[128,1024]{1,0:T(8,128)(2,1)S(1)}, bf16[128,1024]{1,0:T(8,128)(2,1)S(1)}, u32[]{:S(2)}, u32[]{:S(2)}) collective-permute-start(bf16[128,1024]{1,0:T(8,128)(2,1)S(1)} %convert_element_type.112), channel_id=1, source_target_pairs={{0,64},{64,128},{128,192},{192,256},{256,320},{320,384},{384,448},... | collective-permute-start | bytes 786440 | tf_op jit(solution)/shard_map/ppermute | solution.py:22
Sparse Core Ops, SparseCore 0:
  115.4 69.9 reduce-scatter.1
where the time goes:
time: 208 us; the launch traced here: 207 us
  waiting for transfers between devices  111 us (53%)
  local copies, waits for them, and re-layouts  30.3 us (15%)
  matrix products  25.1 us (12%)
  starting transfers between devices  20.3 us (10%)
  between operations  14.3 us (7%)
  other arithmetic  5.93 us (3%)
    reduce_scatter x1, waiting for transfers between devices, body(): lax.psum_scatter(head_term, 'tp', scatter_dimension=1, tiled=True)  70.2 us
    ppermute x3, waiting for transfers between devices, from_behind(): lax.ppermute(value, axis, [(source, source + steps) for source in range(i...  31.5 us
    dot_general x2, local copies, waits for them, and re-layouts, project(): jnp.dot(rows_in, keyval_weight[0], preferred_element_type=jnp.float32)  18.2 us
    ppermute x3, starting transfers between devices, from_behind(): lax.ppermute(value, axis, [(source, source + steps) for source in range(i...  16.8 us
    dot_general x1, local copies, waits for them, and re-layouts, body(): jnp.dot(normed, query_weight[0], preferred_element_type=jnp.float32)  11.3 us
    dot_general x4, matrix products, project(): jnp.dot(rows_in, keyval_weight[0], preferred_element_type=jnp.float32)  10.4 us
    ppermute x1, waiting for transfers between devices, passed_along(): return lax.ppermute(value, axis, pairs)  9.28 us
    dot_general x1, matrix products, body(): jnp.dot(attn, output_weight[0], preferred_element_type=jnp.float32)  6.03 us
  transfers between devices with their start and end apart: 5, of which 3 were waited for; matrix products, arithmetic and copies ran while one was open for 21% of the time, Pallas kernels for 0%

commit v1 on v0

v1 whole, which is shorter than its diff:
```python
import functools

import jax
import jax.numpy as jnp
from jax import lax
from jax.experimental import pallas as pl
from jax.experimental.pallas import tpu as pltpu
from jax.sharding import PartitionSpec as P

HD = 128
NORM_EPS = 1e-05
MESH = pl.DeviceIdType.MESH
LOG2E = 1.4426950408889634


def block_kernel(
    n_seg,
    n_ctx,
    n_tp,
    win_ref,
    gain_ref,
    inv_ref,
    hid_hbm,
    wkv_hbm,
    wq_hbm,
    wo_hbm,
    out_hbm,
    hid,
    wkv,
    wq,
    wo,
    normed,
    kv,
    query,
    attn,
    part,
    landed,
    final,
    load_sem,
    kv_send,
    kv_recv,
    rs_send,
    rs_recv,
    z_send,
    z_recv,
):
    seg = lax.axis_index("segment")
    ctx = lax.axis_index("ctx")
    tp = lax.axis_index("tp")
    rows, width = hid.shape
    heads = query.shape[0]
    groups = kv.shape[2] // (2 * HD)
    per_group = heads // groups
    cols = part.shape[2]

    loads = [
        pltpu.make_async_copy(hid_hbm.at[0], hid, load_sem.at[0]),
        pltpu.make_async_copy(wkv_hbm.at[0], wkv, load_sem.at[1]),
        pltpu.make_async_copy(wq_hbm.at[0], wq, load_sem.at[2]),
        pltpu.make_async_copy(wo_hbm.at[0], wo, load_sem.at[3]),
    ]
    for load in loads:
        load.start()

    def at_ctx(steps):
        return {"ctx": lax.rem(ctx + steps + n_ctx, n_ctx)}

    core = lax.rem(ctx, 2)
    partner = {"ctx": ctx + 1 - 2 * core}

    barrier = pltpu.get_barrier_semaphore()
    peers = [partner]
    peers += [at_ctx(steps) for steps in (2, -2, 3, -3)]
    peers += [{"tp": lax.rem(tp + step, n_tp)} for step in range(1, n_tp)]
    peers += [
        {"segment": lax.rem(seg + 1, n_seg)},
        {"segment": lax.rem(seg + n_seg - 1, n_seg)},
    ]
    for peer in peers:
        pl.semaphore_signal(barrier, inc=1, device_id=peer, device_id_type=MESH)

    row_at = lax.broadcasted_iota(jnp.int32, (rows, HD), 0)
    lane_at = lax.broadcasted_iota(jnp.int32, (rows, HD), 1)
    angles = (ctx * rows + row_at).astype(jnp.float32) * inv_ref[...]
    cosine = jnp.cos(angles)
    sine = jnp.where(lane_at < HD // 2, -jnp.sin(angles), jnp.sin(angles))

    def rope(vector):
        return vector * cosine + pltpu.roll(vector, HD // 2, 1) * sine

    loads[0].wait()
    gain = gain_ref[...].astype(jnp.float32)
    for first in range(0, rows, 16):
        wide = hid[first : first + 16, :].astype(jnp.float32)
        scale = lax.rsqrt(jnp.sum(wide * wide, axis=1, keepdims=True) * (1.0 / width) + NORM_EPS)
        normed[first : first + 16, :] = (wide * scale * gain).astype(jnp.bfloat16)

    loads[1].wait()
    for group in range(groups):
        low = group * 2 * HD
        both = jnp.dot(
            normed[...], wkv[:, low : low + 2 * HD], preferred_element_type=jnp.float32
        )
        kv[0, :, low : low + HD] = rope(both[:, :HD]).astype(jnp.bfloat16)
        kv[0, :, low + HD : low + 2 * HD] = both[:, HD:].astype(jnp.bfloat16)

    pl.semaphore_wait(barrier, len(peers))

    def send_kv(source, slot, target, sem):
        return pltpu.make_async_remote_copy(
            src_ref=kv.at[source],
            dst_ref=kv.at[slot],
            send_sem=kv_send.at[sem],
            recv_sem=kv_recv.at[slot],
            device_id=target,
            device_id_type=MESH,
        )

    across = send_kv(0, 2, at_ctx(2), 0)
    across.start()

    @pl.when(core == 0)
    def _():
        send_kv(0, 1, partner, 1).start()

    @pl.when(core == 1)
    def _():
        send_kv(0, 3, at_ctx(3), 1).start()

    loads[2].wait()

    for pair in range(heads // 2):
        both = jnp.dot(
            normed[...],
            wq[:, pair * 2 * HD : (pair + 1) * 2 * HD],
            preferred_element_type=jnp.float32,
        )
        query[2 * pair] = rope(both[:, :HD]).astype(jnp.bfloat16)
        query[2 * pair + 1] = rope(both[:, HD:]).astype(jnp.bfloat16)

    across.wait_recv()

    @pl.when(core == 0)
    def _():
        send_kv(2, 3, partner, 2).start()

    @pl.when(core == 1)
    def _():
        send_kv(2, 1, partner, 2).start()

    send_kv(0, 1, partner, 1).wait_recv()
    send_kv(0, 3, partner, 2).wait_recv()

    window = win_ref[0]
    biases = []
    for slot in range(4):
        distance = row_at - lane_at + slot * rows
        inside = (distance >= 0) & (distance < window) & (ctx >= slot)
        biases.append(jnp.where(inside, jnp.float32(0.0), jnp.float32(-1e30)))

    for head in range(heads):
        low = (head // per_group) * 2 * HD
        scores = []
        for slot in range(4):
            scores.append(
                lax.dot_general(
                    query[head],
                    kv[slot, :, low : low + HD],
                    (((1,), (1,)), ((), ())),
                    preferred_element_type=jnp.float32,
                )
                + biases[slot]
            )
        highest = jnp.max(
            jnp.maximum(
                jnp.maximum(scores[0], scores[1]), jnp.maximum(scores[2], scores[3])
            ),
            axis=1,
            keepdims=True,
        )
        expo = [jnp.exp2((score - highest) * (HD**-0.5 * LOG2E)) for score in scores]
        total = jnp.sum((expo[0] + expo[1]) + (expo[2] + expo[3]), axis=1, keepdims=True)
        inverse = 1.0 / total
        mixed = None
        for slot in range(4):
            term = jnp.dot(
                (expo[slot] * inverse).astype(jnp.bfloat16),
                kv[slot, :, low + HD : low + 2 * HD],
                preferred_element_type=jnp.float32,
            )
            mixed = term if mixed is None else mixed + term
        attn[:, head * HD : (head + 1) * HD] = mixed.astype(jnp.bfloat16)

    loads[3].wait()

    def share(target):
        low = pl.multiple_of(target * cols, cols)
        return jnp.dot(
            attn[...], wo[:, pl.ds(low, cols)], preferred_element_type=jnp.float32
        )

    sends = []
    for step in range(1, n_tp):
        target = lax.rem(tp + step, n_tp)
        part[step - 1] = share(target).astype(jnp.bfloat16)
        send = pltpu.make_async_remote_copy(
            src_ref=part.at[step - 1],
            dst_ref=landed.at[step - 1],
            send_sem=rs_send.at[step - 1],
            recv_sem=rs_recv.at[step - 1],
            device_id={"tp": target},
            device_id_type=MESH,
        )
        send.start()
        sends.append(send)
    own = share(tp)
    for send in sends:
        send.wait_recv()
    for step in range(n_tp - 1):
        own = own + landed[step].astype(jnp.float32)
    final[...] = own.astype(jnp.bfloat16)
    hand = pltpu.make_async_remote_copy(
        src_ref=final,
        dst_ref=out_hbm.at[0],
        send_sem=z_send,
        recv_sem=z_recv,
        device_id={"segment": lax.rem(seg + 1, n_seg)},
        device_id_type=MESH,
    )
    hand.start()
    across.wait_send()
    send_kv(0, 1, partner, 1).wait_send()
    send_kv(2, 1, partner, 2).wait_send()
    for send in sends:
        send.wait_send()
    hand.wait()


def solution(mesh):
    n_seg, n_ctx, n_tp = mesh.shape["segment"], mesh.shape["ctx"], mesh.shape["tp"]

    def body(hidden_in, norm_gain, query_weight, keyval_weight, output_weight, windows):
        rows, width = hidden_in.shape[1:]
        heads = query_weight.shape[2] // HD
        cols = output_weight.shape[2] // n_tp
        half = HD // 2
        inverse = 10000.0 ** (-jnp.arange(half, dtype=jnp.float32) / half)
        inverse = jnp.concatenate([inverse, inverse])[None, :]
        bf16 = jnp.bfloat16
        vmem = pl.BlockSpec(memory_space=pltpu.VMEM)
        hbm = pl.BlockSpec(memory_space=pl.ANY)
        return pl.pallas_call(
            functools.partial(block_kernel, n_seg, n_ctx, n_tp),
            out_shape=jax.ShapeDtypeStruct((1, rows, cols), bf16),
            in_specs=[pl.BlockSpec(memory_space=pltpu.SMEM), vmem, vmem, hbm, hbm, hbm, hbm],
            out_specs=hbm,
            scratch_shapes=[
                pltpu.VMEM((rows, width), bf16),
                pltpu.VMEM(keyval_weight.shape[1:], bf16),
                pltpu.VMEM(query_weight.shape[1:], bf16),
                pltpu.VMEM(output_weight.shape[1:], bf16),
                pltpu.VMEM((rows, width), bf16),
                pltpu.VMEM((4, rows, keyval_weight.shape[2]), bf16),
                pltpu.VMEM((heads, rows, HD), bf16),
                pltpu.VMEM((rows, heads * HD), bf16),
                pltpu.VMEM((n_tp - 1, rows, cols), bf16),
                pltpu.VMEM((n_tp - 1, rows, cols), bf16),
                pltpu.VMEM((rows, cols), bf16),
                pltpu.SemaphoreType.DMA((4,)),
                pltpu.SemaphoreType.DMA((3,)),
                pltpu.SemaphoreType.DMA((4,)),
                pltpu.SemaphoreType.DMA((n_tp - 1,)),
                pltpu.SemaphoreType.DMA((n_tp - 1,)),
                pltpu.SemaphoreType.DMA,
                pltpu.SemaphoreType.DMA,
            ],
            compiler_params=pltpu.CompilerParams(
                collective_id=0, has_side_effects=True, vmem_limit_bytes=56 * 1024 * 1024
            ),
        )(
            windows,
            norm_gain,
            inverse,
            hidden_in,
            keyval_weight,
            query_weight,
            output_weight,
        )

    in_specs = (
        P("segment", "ctx", None),
        P("segment", None),
        P("segment", None, "tp"),
        P("segment", None, "tp"),
        P("segment", "tp", None),
        P("segment"),
    )
    out_specs = P("segment", "ctx", "tp")
    return jax.shard_map(body, mesh=mesh, in_specs=in_specs, out_specs=out_specs, check_vma=False)
```

time: 208 us -> 70.1 us (0.34)
  the two profiles are of different devices: /device:TPU:56 before, /device:TPU:24 now
where the time goes in v1:
time: 70.1 us; the launch traced here: 69.9 us
  Pallas kernels  66.9 us (95%)
  local copies, waits for them, and re-layouts  1.67 us (2%)
    pallas_call x1, Pallas kernels, body(): pl.pallas_call(functools.partial(block_kernel, n_seg, n_ctx, n_tp), out_s...  66.9 us
    unnamed x1, local copies, waits for them, and re-layouts  1.67 us

profile of v1, /device:TPU:24, one launch (start us, length us, event | category | flops | bytes accessed | tf_op | source)
XLA Modules:
  0.0 69.9 jit_solution(8771787596145149811)
XLA Ops:
  0.7 0.6 maximum_bitcast_fusion.inv_ref
  1.3 66.9 %shard_map.64 = bf16[1,128,1024]{2,1,0:T(8,128)(2,1)} custom-call(s32[1]{0:T(128)S(6)} %copy.8.win_ref, bf16[1,4096]{1,0:T(2,128)(2,1)} %gain_ref.1, f32[1,128]{1,0:T(1,128)} %maximum_bitcast_fusion.inv_ref, bf16[1,128,4096]{2,1,0:T(8,128)(2,1)} %hid_hbm.1, bf16[1,4096,512]{2,1,0:T(8,128)(2,1)} %wkv_hbm.1, bf16[1,4096,1024]{2,1,0:T(8,128)(2,1)} %wq_hbm.1, ...), custom_call_target="tpu_custom_call" | custom-call | tf_op jit(solution)/shard_map/pallas_call | solution.py:252
  68.2 1.7 %copy.9 = bf16[1,128,1024]{2,1,0:T(8,128)(2,1)} copy(bf16[1,128,1024]{2,1,0:T(8,128)(2,1)} %shard_map.64) | data formatting | bytes 524288
  (1 shorter events, 0.0 us)

commit v2 on v1

v2 whole, which is shorter than its diff:
```python
import functools

import jax
import jax.numpy as jnp
import numpy as np
from jax import lax
from jax.experimental import pallas as pl
from jax.experimental.pallas import tpu as pltpu
from jax.sharding import PartitionSpec as P

HD = 128
PIECE = 32
NORM_EPS = 1e-05
MESH = pl.DeviceIdType.MESH
LOG2E = 1.4426950408889634


def block_kernel(
    n_seg,
    n_ctx,
    n_tp,
    piece,
    win_ref,
    gain_ref,
    inv_ref,
    hid_hbm,
    wkv_hbm,
    wq_hbm,
    wo_hbm,
    out_hbm,
    hid,
    wkv,
    wq,
    wo,
    normed,
    kv,
    query,
    attn,
    bias,
    own,
    part,
    from_outer,
    from_inner,
    final,
    load_sem,
    kv_send,
    kv_recv,
    rs_send,
    outer_recv,
    inner_recv,
    z_send,
    z_recv,
):
    seg = lax.axis_index("segment")
    ctx = lax.axis_index("ctx")
    tp = lax.axis_index("tp")
    rows, width = hid.shape
    heads = query.shape[0]
    groups = kv.shape[1]
    per_group = heads // groups
    cols = part.shape[2]

    loads = [
        pltpu.make_async_copy(hid_hbm.at[0], hid, load_sem.at[0]),
        pltpu.make_async_copy(wkv_hbm.at[0], wkv, load_sem.at[1]),
        pltpu.make_async_copy(wq_hbm.at[0], wq, load_sem.at[2]),
        pltpu.make_async_copy(wo_hbm.at[0], wo, load_sem.at[3]),
    ]
    loads[0].start()
    loads[1].start()

    def at_ctx(steps):
        return {"ctx": lax.rem(ctx + steps + n_ctx, n_ctx)}

    core = lax.rem(ctx, 2)
    partner = {"ctx": ctx + 1 - 2 * core}
    half = tp // 2
    inward = {"tp": tp + 1 - 2 * half}
    at_end = lax.rem(tp, 3) == 0

    barrier = pltpu.get_barrier_semaphore()
    peers = [partner]
    peers += [at_ctx(steps) for steps in (2, -2, 3, -3)]
    peers += [{"tp": lax.rem(tp + step, n_tp)} for step in range(1, n_tp)]
    peers += [
        {"segment": lax.rem(seg + 1, n_seg)},
        {"segment": lax.rem(seg + n_seg - 1, n_seg)},
    ]
    for peer in peers:
        pl.semaphore_signal(barrier, inc=1, device_id=peer, device_id_type=MESH)

    row_at = lax.broadcasted_iota(jnp.int32, (rows, HD), 0)
    lane_at = lax.broadcasted_iota(jnp.int32, (rows, HD), 1)
    angles = (ctx * rows + row_at).astype(jnp.float32) * inv_ref[...]
    cosine = jnp.cos(angles)
    sine = jnp.sin(angles)
    sine = jnp.where(lane_at < HD // 2, -sine, sine)

    def rope(vector):
        return vector * cosine + pltpu.roll(vector, HD // 2, 1) * sine

    loads[0].wait()
    loads[2].start()
    loads[3].start()
    gain = gain_ref[...].astype(jnp.float32)
    for first in range(0, rows, 16):
        wide = hid[first : first + 16, :].astype(jnp.float32)
        scale = lax.rsqrt(jnp.sum(wide * wide, axis=1, keepdims=True) * (1.0 / width) + NORM_EPS)
        normed[first : first + 16, :] = (wide * scale * gain).astype(jnp.bfloat16)

    def send_kv(source, slot, group, target, sem):
        return pltpu.make_async_remote_copy(
            src_ref=kv.at[source, group],
            dst_ref=kv.at[slot, group],
            send_sem=kv_send.at[sem, group],
            recv_sem=kv_recv.at[slot, group],
            device_id=target,
            device_id_type=MESH,
        )

    loads[1].wait()
    for group in range(groups):
        low = group * 2 * HD
        both = jnp.dot(
            normed[...], wkv[:, low : low + 2 * HD], preferred_element_type=jnp.float32
        )
        kv[0, group, :, :HD] = rope(both[:, :HD]).astype(jnp.bfloat16)
        kv[0, group, :, HD:] = both[:, HD:].astype(jnp.bfloat16)
        if group == 0:
            pl.semaphore_wait(barrier, len(peers))
        send_kv(0, 2, group, at_ctx(2), 0).start()

        @pl.when(core == 0)
        def _():
            send_kv(0, 1, group, partner, 1).start()

        @pl.when(core == 1)
        def _():
            send_kv(0, 3, group, at_ctx(3), 1).start()

    loads[2].wait()

    for pair in range(heads // 2):
        both = jnp.dot(
            normed[...],
            wq[:, pair * 2 * HD : (pair + 1) * 2 * HD],
            preferred_element_type=jnp.float32,
        )
        query[2 * pair] = rope(both[:, :HD]).astype(jnp.bfloat16)
        query[2 * pair + 1] = rope(both[:, HD:]).astype(jnp.bfloat16)

    window = win_ref[0]
    for slot in range(4):
        distance = row_at - lane_at + slot * rows
        inside = (distance >= 0) & (distance < window) & (ctx >= slot)
        bias[slot] = jnp.where(inside, jnp.float32(0.0), jnp.float32(-1e30))

    for group in range(groups):
        send_kv(0, 2, group, partner, 0).wait_recv()

        @pl.when(core == 0)
        def _():
            send_kv(2, 3, group, partner, 2).start()

        @pl.when(core == 1)
        def _():
            send_kv(2, 1, group, partner, 2).start()

    for group in range(groups):
        send_kv(0, 1, group, partner, 1).wait_recv()
        send_kv(0, 3, group, partner, 2).wait_recv()
        for head in range(group * per_group, (group + 1) * per_group):
            scores = []
            for slot in range(4):
                scores.append(
                    lax.dot_general(
                        query[head],
                        kv[slot, group, :, :HD],
                        (((1,), (1,)), ((), ())),
                        preferred_element_type=jnp.float32,
                    )
                    + bias[slot]
                )
            highest = jnp.max(
                jnp.maximum(
                    jnp.maximum(scores[0], scores[1]), jnp.maximum(scores[2], scores[3])
                ),
                axis=1,
                keepdims=True,
            )
            expo = [jnp.exp2((score - highest) * (HD**-0.5 * LOG2E)) for score in scores]
            total = jnp.sum((expo[0] + expo[1]) + (expo[2] + expo[3]), axis=1, keepdims=True)
            inverse = 1.0 / total
            mixed = None
            for slot in range(4):
                term = jnp.dot(
                    (expo[slot] * inverse).astype(jnp.bfloat16),
                    kv[slot, group, :, HD:],
                    preferred_element_type=jnp.float32,
                )
                mixed = term if mixed is None else mixed + term
            attn[:, head * HD : (head + 1) * HD] = mixed.astype(jnp.bfloat16)

    loads[3].wait()

    def send_part(index, at, place, sem, target):
        band = pl.ds(at * piece, piece)
        return pltpu.make_async_remote_copy(
            src_ref=part.at[index, band],
            dst_ref=place.at[band],
            send_sem=rs_send.at[index, at],
            recv_sem=sem.at[at],
            device_id=target,
            device_id_type=MESH,
        )

    def to_inner(index, at):
        return send_part(index, at, from_outer.at[index], outer_recv.at[index], inward)

    def over_middle(index, at):
        return send_part(index, at, from_inner.at[index], inner_recv.at[index], inward)

    def to_end(at):
        outward = {"tp": tp - 1 + 2 * half}
        return send_part(2, at, from_inner.at[0], inner_recv.at[0], outward)

    def hand(at):
        band = pl.ds(at * piece, piece)
        return pltpu.make_async_remote_copy(
            src_ref=final.at[band],
            dst_ref=out_hbm.at[0, band],
            send_sem=z_send.at[at],
            recv_sem=z_recv.at[at],
            device_id={"segment": lax.rem(seg + 1, n_seg)},
            device_id_type=MESH,
        )

    f32 = jnp.float32
    bands = rows // piece
    for step in range(4):
        mirrored = 3 - step
        low = pl.multiple_of((mirrored + half * (3 - 2 * mirrored)) * cols, cols)
        share = jnp.dot(attn[...], wo[:, pl.ds(low, cols)], preferred_element_type=f32)
        own[step] = share
        if step < 3:

            @pl.when(at_end)
            def _():
                part[step] = share.astype(jnp.bfloat16)
                for at in range(bands):
                    to_inner(step, at).start()

    def finish(at, terms):
        band = slice(at * piece, (at + 1) * piece)
        total = terms[0][band]
        for term in terms[1:]:
            total = total + term[band].astype(f32)
        final[band] = total.astype(jnp.bfloat16)
        hand(at).start()

    def add_on(index, at, mine, landed):
        band = slice(at * piece, (at + 1) * piece)
        part[index, band] = (mine[band] + landed[band].astype(f32)).astype(jnp.bfloat16)

    @pl.when(at_end)
    def _():
        for at in range(bands):
            to_end(at).wait_recv()
            finish(at, [own.at[3], from_inner.at[0]])
        for step in range(3):
            for at in range(bands):
                to_inner(step, at).wait_send()

    @pl.when(jnp.logical_not(at_end))
    def _():
        for at in range(bands):
            to_inner(0, at).wait_recv()
            add_on(0, at, own.at[0], from_outer.at[0])
            over_middle(0, at).start()
        for at in range(bands):
            to_inner(1, at).wait_recv()
            add_on(1, at, own.at[1], from_outer.at[1])
            over_middle(1, at).start()
            over_middle(0, at).wait_recv()
            add_on(2, at, own.at[3], from_inner.at[0])
            to_end(at).start()
        for at in range(bands):
            to_inner(2, at).wait_recv()
            over_middle(1, at).wait_recv()
            finish(at, [own.at[2], from_outer.at[2], from_inner.at[1]])
        for at in range(bands):
            over_middle(0, at).wait_send()
            over_middle(1, at).wait_send()
            to_end(at).wait_send()

    for group in range(groups):
        send_kv(0, 2, group, partner, 0).wait_send()
        send_kv(0, 1, group, partner, 1).wait_send()
        send_kv(2, 1, group, partner, 2).wait_send()
    for at in range(bands):
        hand(at).wait()


def solution(mesh):
    n_seg, n_ctx, n_tp = mesh.shape["segment"], mesh.shape["ctx"], mesh.shape["tp"]

    def body(hidden_in, norm_gain, query_weight, keyval_weight, output_weight, windows):
        rows, width = hidden_in.shape[1:]
        heads = query_weight.shape[2] // HD
        cols = output_weight.shape[2] // n_tp
        groups = keyval_weight.shape[2] // (2 * HD)
        bands = rows // PIECE
        half = HD // 2
        inverse = 10000.0 ** (-np.arange(half) / half)
        inverse = jnp.asarray(np.tile(inverse, 2)[None, :], dtype=jnp.float32)
        bf16 = jnp.bfloat16
        vmem = pl.BlockSpec(memory_space=pltpu.VMEM)
        hbm = pl.BlockSpec(memory_space=pl.ANY)
        return pl.pallas_call(
            functools.partial(block_kernel, n_seg, n_ctx, n_tp, PIECE),
            out_shape=jax.ShapeDtypeStruct((1, rows, cols), bf16),
            in_specs=[pl.BlockSpec(memory_space=pltpu.SMEM), vmem, vmem, hbm, hbm, hbm, hbm],
            out_specs=hbm,
            scratch_shapes=[
                pltpu.VMEM((rows, width), bf16),
                pltpu.VMEM(keyval_weight.shape[1:], bf16),
                pltpu.VMEM(query_weight.shape[1:], bf16),
                pltpu.VMEM(output_weight.shape[1:], bf16),
                pltpu.VMEM((rows, width), bf16),
                pltpu.VMEM((4, groups, rows, 2 * HD), bf16),
                pltpu.VMEM((heads, rows, HD), bf16),
                pltpu.VMEM((rows, heads * HD), bf16),
                pltpu.VMEM((4, rows, HD), jnp.float32),
                pltpu.VMEM((4, rows, cols), jnp.float32),
                pltpu.VMEM((3, rows, cols), bf16),
                pltpu.VMEM((3, rows, cols), bf16),
                pltpu.VMEM((2, rows, cols), bf16),
                pltpu.VMEM((rows, cols), bf16),
                pltpu.SemaphoreType.DMA((4,)),
                pltpu.SemaphoreType.DMA((3, groups)),
                pltpu.SemaphoreType.DMA((4, groups)),
                pltpu.SemaphoreType.DMA((3, bands)),
                pltpu.SemaphoreType.DMA((3, bands)),
                pltpu.SemaphoreType.DMA((2, bands)),
                pltpu.SemaphoreType.DMA((bands,)),
                pltpu.SemaphoreType.DMA((bands,)),
            ],
            compiler_params=pltpu.CompilerParams(
                collective_id=0, has_side_effects=True, vmem_limit_bytes=56 * 1024 * 1024
            ),
        )(
            windows,
            norm_gain,
            inverse,
            hidden_in,
            keyval_weight,
            query_weight,
            output_weight,
        )

    in_specs = (
        P("segment", "ctx", None),
        P("segment", None),
        P("segment", None, "tp"),
        P("segment", None, "tp"),
        P("segment", "tp", None),
        P("segment"),
    )
    out_specs = P("segment", "ctx", "tp")
    return jax.shard_map(body, mesh=mesh, in_specs=in_specs, out_specs=out_specs, check_vma=False)
```

time: 70.1 us -> 60 us (0.86)
  the two profiles are of different devices: /device:TPU:24 before, /device:TPU:8 now
where the time goes in v2:
time: 60 us; the launch traced here: 59.8 us
  Pallas kernels  57.5 us (96%)
  local copies, waits for them, and re-layouts  1.67 us (3%)
  between operations  0.66 us (1%)
    pallas_call x1, Pallas kernels, body(): pl.pallas_call(functools.partial(block_kernel, n_seg, n_ctx, n_tp, PIECE)...  57.5 us
    unnamed x1, local copies, waits for them, and re-layouts  1.67 us

profile of v2, /device:TPU:8, one launch (start us, length us, event | category | flops | bytes accessed | tf_op | source)
XLA Modules:
  0.0 59.8 jit_solution(6356363733149361802)
XLA Ops:
  0.7 57.5 %shard_map.73 = bf16[1,128,1024]{2,1,0:T(8,128)(2,1)} custom-call(s32[1]{0:T(128)S(6)} %copy.9.win_ref, bf16[1,4096]{1,0:T(2,128)(2,1)} %gain_ref.1, f32[1,128]{1,0:T(1,128)} %constant.2.clone.inv_ref, bf16[1,128,4096]{2,1,0:T(8,128)(2,1)} %hid_hbm.1, bf16[1,4096,512]{2,1,0:T(8,128)(2,1)} %wkv_hbm.1, bf16[1,4096,1024]{2,1,0:T(8,128)(2,1)} %wq_hbm.1, ...), custom_call_target="tpu_custom_call" | custom-call | tf_op jit(solution)/shard_map/pallas_call | solution.py:319
  58.2 1.7 %copy.10 = bf16[1,128,1024]{2,1,0:T(8,128)(2,1)} copy(bf16[1,128,1024]{2,1,0:T(8,128)(2,1)} %shard_map.73) | data formatting | bytes 524288

commit v3 on v2

--- a/solution.py
+++ b/solution.py
@@ -9,7 +9,8 @@
 from jax.sharding import PartitionSpec as P
 
 HD = 128
-PIECE = 32
+PIECE = 16
+DEPTHS = 4
 NORM_EPS = 1e-05
 MESH = pl.DeviceIdType.MESH
 LOG2E = 1.4426950408889634
@@ -21,13 +22,15 @@
     n_tp,
     piece,
     win_ref,
-    gain_ref,
-    inv_ref,
+    gain_hbm,
+    inv_hbm,
     hid_hbm,
     wkv_hbm,
     wq_hbm,
     wo_hbm,
-    out_hbm,
+    out_ref,
+    gain_row,
+    inv_row,
     hid,
     wkv,
     wq,
@@ -60,14 +63,22 @@
     per_group = heads // groups
     cols = part.shape[2]
 
-    loads = [
-        pltpu.make_async_copy(hid_hbm.at[0], hid, load_sem.at[0]),
-        pltpu.make_async_copy(wkv_hbm.at[0], wkv, load_sem.at[1]),
-        pltpu.make_async_copy(wq_hbm.at[0], wq, load_sem.at[2]),
-        pltpu.make_async_copy(wo_hbm.at[0], wo, load_sem.at[3]),
+    depth = width // DEPTHS
+    small = [
+        pltpu.make_async_copy(inv_hbm, inv_row, load_sem.at[0]),
+        pltpu.make_async_copy(gain_hbm, gain_row, load_sem.at[1]),
     ]
-    loads[0].start()
-    loads[1].start()
+    load_hid = pltpu.make_async_copy(hid_hbm.at[0], hid, load_sem.at[2])
+    load_wq = pltpu.make_async_copy(wq_hbm.at[0], wq, load_sem.at[3])
+    load_wo = pltpu.make_async_copy(wo_hbm.at[0], wo, load_sem.at[4])
+    load_wkv = []
+    for at in range(DEPTHS):
+        band = pl.ds(at * depth, depth)
+        load_wkv.append(
+            pltpu.make_async_copy(wkv_hbm.at[0, band], wkv.at[band], load_sem.at[5 + at])
+        )
+    for load in small + [load_hid] + load_wkv:
+        load.start()
 
     def at_ctx(steps):
         return {"ctx": lax.rem(ctx + steps + n_ctx, n_ctx)}
@@ -89,9 +100,10 @@
     for peer in peers:
         pl.semaphore_signal(barrier, inc=1, device_id=peer, device_id_type=MESH)
 
+    small[0].wait()
     row_at = lax.broadcasted_iota(jnp.int32, (rows, HD), 0)
     lane_at = lax.broadcasted_iota(jnp.int32, (rows, HD), 1)
-    angles = (ctx * rows + row_at).astype(jnp.float32) * inv_ref[...]
+    angles = (ctx * rows + row_at).astype(jnp.float32) * inv_row[...]
     cosine = jnp.cos(angles)
     sine = jnp.sin(angles)
     sine = jnp.where(lane_at < HD // 2, -sine, sine)
@@ -99,10 +111,9 @@
     def rope(vector):
         return vector * cosine + pltpu.roll(vector, HD // 2, 1) * sine
 
-    loads[0].wait()
-    loads[2].start()
-    loads[3].start()
-    gain = gain_ref[...].astype(jnp.float32)
+    small[1].wait()
+    load_hid.wait()
+    gain = gain_row[...].astype(jnp.float32)
     for first in range(0, rows, 16):
         wide = hid[first : first + 16, :].astype(jnp.float32)
         scale = lax.rsqrt(jnp.sum(wide * wide, axis=1, keepdims=True) * (1.0 / width) + NORM_EPS)
@@ -118,16 +129,18 @@
             device_id_type=MESH,
         )
 
-    loads[1].wait()
+    both = None
+    for at in range(DEPTHS):
+        band = slice(at * depth, (at + 1) * depth)
+        load_wkv[at].wait()
+        term = jnp.dot(normed[:, band], wkv[band, :], preferred_element_type=jnp.float32)
+        both = term if both is None else both + term
     for group in range(groups):
         low = group * 2 * HD
-        both = jnp.dot(
-            normed[...], wkv[:, low : low + 2 * HD], preferred_element_type=jnp.float32
-        )
-        kv[0, group, :, :HD] = rope(both[:, :HD]).astype(jnp.bfloat16)
-        kv[0, group, :, HD:] = both[:, HD:].astype(jnp.bfloat16)
-        if group == 0:
-            pl.semaphore_wait(barrier, len(peers))
+        kv[0, group, :, :HD] = rope(both[:, low : low + HD]).astype(jnp.bfloat16)
+        kv[0, group, :, HD:] = both[:, low + HD : low + 2 * HD].astype(jnp.bfloat16)
+    pl.semaphore_wait(barrier, len(peers))
+    for group in range(groups):
         send_kv(0, 2, group, at_ctx(2), 0).start()
 
         @pl.when(core == 0)
@@ -138,7 +151,9 @@
         def _():
             send_kv(0, 3, group, at_ctx(3), 1).start()
 
-    loads[2].wait()
+    load_wq.start()
+    load_wo.start()
+    load_wq.wait()
 
     for pair in range(heads // 2):
         both = jnp.dot(
@@ -201,7 +216,7 @@
                 mixed = term if mixed is None else mixed + term
             attn[:, head * HD : (head + 1) * HD] = mixed.astype(jnp.bfloat16)
 
-    loads[3].wait()
+    load_wo.wait()
 
     def send_part(index, at, place, sem, target):
         band = pl.ds(at * piece, piece)
@@ -228,7 +243,7 @@
         band = pl.ds(at * piece, piece)
         return pltpu.make_async_remote_copy(
             src_ref=final.at[band],
-            dst_ref=out_hbm.at[0, band],
+            dst_ref=out_ref.at[0, band],
             send_sem=z_send.at[at],
             recv_sem=z_recv.at[at],
             device_id={"segment": lax.rem(seg + 1, n_seg)},
@@ -318,10 +333,12 @@
         hbm = pl.BlockSpec(memory_space=pl.ANY)
         return pl.pallas_call(
             functools.partial(block_kernel, n_seg, n_ctx, n_tp, PIECE),
-            out_shape=jax.ShapeDtypeStruct((1, rows, cols), bf16),
-            in_specs=[pl.BlockSpec(memory_space=pltpu.SMEM), vmem, vmem, hbm, hbm, hbm, hbm],
-            out_specs=hbm,
+            out_shape=pltpu.VMEM((1, rows, cols), bf16),
+            in_specs=[pl.BlockSpec(memory_space=pltpu.SMEM)] + [hbm] * 6,
+            out_specs=vmem,
             scratch_shapes=[
+                pltpu.VMEM((1, width), bf16),
+                pltpu.VMEM((1, HD), jnp.float32),
                 pltpu.VMEM((rows, width), bf16),
                 pltpu.VMEM(keyval_weight.shape[1:], bf16),
                 pltpu.VMEM(query_weight.shape[1:], bf16),
@@ -336,7 +353,7 @@
                 pltpu.VMEM((3, rows, cols), bf16),
                 pltpu.VMEM((2, rows, cols), bf16),
                 pltpu.VMEM((rows, cols), bf16),
-                pltpu.SemaphoreType.DMA((4,)),
+                pltpu.SemaphoreType.DMA((5 + DEPTHS,)),
                 pltpu.SemaphoreType.DMA((3, groups)),
                 pltpu.SemaphoreType.DMA((4, groups)),
                 pltpu.SemaphoreType.DMA((3, bands)),

time: 60 us -> 57.7 us (0.962)
  Pallas kernels: 57.5 us -> 56.2 us
  local copies, waits for them, and re-layouts: 1.67 us -> 0.71 us
    pallas_call x1, Pallas kernels: 57.5 us -> 56.2 us  [body(): pl.pallas_call(functools.partial(block_kernel, n_seg, n_ctx, n_tp, PIECE)...]
    unnamed x1, local copies, waits for them, and re-layouts: 1.67 us -> 0.71 us
where the time goes in v3:
time: 57.7 us; the launch traced here: 57.6 us
  Pallas kernels  56.2 us (97%)
  local copies, waits for them, and re-layouts  0.71 us (1%)
  between operations  0.66 us (1%)
    pallas_call x1, Pallas kernels, body(): pl.pallas_call(functools.partial(block_kernel, n_seg, n_ctx, n_tp, PIECE)...  56.2 us

profile of v3, /device:TPU:8, one launch (start us, length us, event | category | flops | bytes accessed | tf_op | source)
XLA Modules:
  0.0 57.6 jit_solution(694500704208975642)
XLA Ops:
  0.7 56.2 %shard_map.73 = bf16[1,128,1024]{2,1,0:T(8,128)(2,1)S(1)} custom-call(s32[1]{0:T(128)S(6)} %copy.10.win_ref, bf16[1,4096]{1,0:T(2,128)(2,1)} %gain_hbm.1, f32[1,128]{1,0:T(1,128)} %constant.2.clone.inv_hbm, bf16[1,128,4096]{2,1,0:T(8,128)(2,1)} %hid_hbm.1, bf16[1,4096,512]{2,1,0:T(8,128)(2,1)} %wkv_hbm.1, bf16[1,4096,1024]{2,1,0:T(8,128)(2,1)} %wq_hbm.1, ...), custom_call_target="tpu_custom_call" | custom-call | tf_op jit(solution)/shard_map/pallas_call | solution.py:334
  56.9 0.7 %copy.9 = bf16[1,128,1024]{2,1,0:T(8,128)(2,1)} copy(bf16[1,128,1024]{2,1,0:T(8,128)(2,1)S(1)} %shard_map.73) | data formatting | bytes 524288

commit v4 on v3

--- a/solution.py
+++ b/solution.py
@@ -38,12 +38,15 @@
     normed,
     kv,
     query,
+    probs,
     attn,
     bias,
     own,
     part,
     from_outer,
     from_inner,
+    from_mate,
+    from_behind,
     final,
     load_sem,
     kv_send,
@@ -51,6 +54,7 @@
     rs_send,
     outer_recv,
     inner_recv,
+    mate_recv,
     z_send,
     z_recv,
 ):
@@ -59,7 +63,7 @@
     tp = lax.axis_index("tp")
     rows, width = hid.shape
     heads = query.shape[0]
-    groups = kv.shape[1]
+    groups = kv.shape[1] // 2
     per_group = heads // groups
     cols = part.shape[2]
 
@@ -87,6 +91,7 @@
     partner = {"ctx": ctx + 1 - 2 * core}
     half = tp // 2
     inward = {"tp": tp + 1 - 2 * half}
+    mate = tp + 1 - 2 * lax.rem(tp, 2)
     at_end = lax.rem(tp, 3) == 0
 
     barrier = pltpu.get_barrier_semaphore()
@@ -96,6 +101,8 @@
     peers += [
         {"segment": lax.rem(seg + 1, n_seg)},
         {"segment": lax.rem(seg + n_seg - 1, n_seg)},
+        {"segment": lax.rem(seg + 1, n_seg), "tp": mate},
+        {"segment": lax.rem(seg + n_seg - 1, n_seg), "tp": mate},
     ]
     for peer in peers:
         pl.semaphore_signal(barrier, inc=1, device_id=peer, device_id_type=MESH)
@@ -137,19 +144,19 @@
         both = term if both is None else both + term
     for group in range(groups):
         low = group * 2 * HD
-        kv[0, group, :, :HD] = rope(both[:, low : low + HD]).astype(jnp.bfloat16)
-        kv[0, group, :, HD:] = both[:, low + HD : low + 2 * HD].astype(jnp.bfloat16)
+        kv[0, group] = rope(both[:, low : low + HD]).astype(jnp.bfloat16)
+        kv[0, groups + group] = both[:, low + HD : low + 2 * HD].astype(jnp.bfloat16)
     pl.semaphore_wait(barrier, len(peers))
-    for group in range(groups):
-        send_kv(0, 2, group, at_ctx(2), 0).start()
+    for part_at in range(2 * groups):
+        send_kv(0, 2, part_at, at_ctx(2), 0).start()
 
         @pl.when(core == 0)
         def _():
-            send_kv(0, 1, group, partner, 1).start()
+            send_kv(0, 1, part_at, partner, 1).start()
 
         @pl.when(core == 1)
         def _():
-            send_kv(0, 3, group, at_ctx(3), 1).start()
+            send_kv(0, 3, part_at, at_ctx(3), 1).start()
 
     load_wq.start()
     load_wo.start()
@@ -170,27 +177,29 @@
         inside = (distance >= 0) & (distance < window) & (ctx >= slot)
         bias[slot] = jnp.where(inside, jnp.float32(0.0), jnp.float32(-1e30))
 
-    for group in range(groups):
-        send_kv(0, 2, group, partner, 0).wait_recv()
+    def pass_on(part_at):
+        send_kv(0, 2, part_at, partner, 0).wait_recv()
 
         @pl.when(core == 0)
         def _():
-            send_kv(2, 3, group, partner, 2).start()
+            send_kv(2, 3, part_at, partner, 2).start()
 
         @pl.when(core == 1)
         def _():
-            send_kv(2, 1, group, partner, 2).start()
-
-    for group in range(groups):
-        send_kv(0, 1, group, partner, 1).wait_recv()
-        send_kv(0, 3, group, partner, 2).wait_recv()
+            send_kv(2, 1, part_at, partner, 2).start()
+
+    def here(part_at):
+        send_kv(0, 1, part_at, partner, 1).wait_recv()
+        send_kv(0, 3, part_at, partner, 2).wait_recv()
+
+    def weigh(group):
         for head in range(group * per_group, (group + 1) * per_group):
             scores = []
             for slot in range(4):
                 scores.append(
                     lax.dot_general(
                         query[head],
-                        kv[slot, group, :, :HD],
+                        kv[slot, group],
                         (((1,), (1,)), ((), ())),
                         preferred_element_type=jnp.float32,
                     )
@@ -206,17 +215,34 @@
             expo = [jnp.exp2((score - highest) * (HD**-0.5 * LOG2E)) for score in scores]
             total = jnp.sum((expo[0] + expo[1]) + (expo[2] + expo[3]), axis=1, keepdims=True)
             inverse = 1.0 / total
+            for slot in range(4):
+                probs[head, slot] = (expo[slot] * inverse).astype(jnp.bfloat16)
+
+    def mix(group):
+        for head in range(group * per_group, (group + 1) * per_group):
             mixed = None
             for slot in range(4):
                 term = jnp.dot(
-                    (expo[slot] * inverse).astype(jnp.bfloat16),
-                    kv[slot, group, :, HD:],
-                    preferred_element_type=jnp.float32,
+                    probs[head, slot], kv[slot, groups + group], preferred_element_type=jnp.float32
                 )
                 mixed = term if mixed is None else mixed + term
             attn[:, head * HD : (head + 1) * HD] = mixed.astype(jnp.bfloat16)
 
+    for part_at in range(groups):
+        pass_on(part_at)
+    for group in range(groups):
+        here(group)
+        weigh(group)
+        pass_on(groups + group)
+    for group in range(groups):
+        here(groups + group)
+        mix(group)
+
     load_wo.wait()
+
+    bands = rows // piece
+    ahead_too = seg == n_seg - 1
+    from_last = seg == 0
 
     def send_part(index, at, place, sem, target):
         band = pl.ds(at * piece, piece)
@@ -239,6 +265,26 @@
         outward = {"tp": tp - 1 + 2 * half}
         return send_part(2, at, from_inner.at[0], inner_recv.at[0], outward)
 
+    def skip_ahead(at):
+        return pltpu.make_async_remote_copy(
+            src_ref=part.at[2, pl.ds(at * piece, piece)],
+            dst_ref=from_mate.at[at],
+            send_sem=rs_send.at[2, at],
+            recv_sem=mate_recv.at[at],
+            device_id={"segment": lax.rem(seg + 1, n_seg), "tp": mate},
+            device_id_type=MESH,
+        )
+
+    def rest_ahead(at):
+        return pltpu.make_async_remote_copy(
+            src_ref=final.at[pl.ds(at * piece, piece)],
+            dst_ref=from_behind.at[at],
+            send_sem=z_send.at[at],
+            recv_sem=z_recv.at[at],
+            device_id={"segment": lax.rem(seg + 1, n_seg)},
+            device_id_type=MESH,
+        )
+
     def hand(at):
         band = pl.ds(at * piece, piece)
         return pltpu.make_async_remote_copy(
@@ -251,7 +297,6 @@
         )
 
     f32 = jnp.float32
-    bands = rows // piece
     for step in range(4):
         mirrored = 3 - step
         low = pl.multiple_of((mirrored + half * (3 - 2 * mirrored)) * cols, cols)
@@ -262,8 +307,20 @@
             @pl.when(at_end)
             def _():
                 part[step] = share.astype(jnp.bfloat16)
-                for at in range(bands):
-                    to_inner(step, at).start()
+                if step < 2:
+                    for at in range(bands):
+                        to_inner(step, at).start()
+                else:
+
+                    @pl.when(ahead_too)
+                    def _():
+                        for at in range(bands):
+                            skip_ahead(at).start()
+
+                    @pl.when(jnp.logical_not(ahead_too))
+                    def _():
+                        for at in range(bands):
+                            to_inner(2, at).start()
 
     def finish(at, terms):
         band = slice(at * piece, (at + 1) * piece)
@@ -285,6 +342,8 @@
         for step in range(3):
             for at in range(bands):
                 to_inner(step, at).wait_send()
+        for at in range(bands):
+            hand(at).wait()
 
     @pl.when(jnp.logical_not(at_end))
     def _():
@@ -299,21 +358,48 @@
             over_middle(0, at).wait_recv()
             add_on(2, at, own.at[3], from_inner.at[0])
             to_end(at).start()
-        for at in range(bands):
-            to_inner(2, at).wait_recv()
-            over_middle(1, at).wait_recv()
-            finish(at, [own.at[2], from_outer.at[2], from_inner.at[1]])
+
+        @pl.when(ahead_too)
+        def _():
+            for at in range(bands):
+                over_middle(1, at).wait_recv()
+                band = slice(at * piece, (at + 1) * piece)
+                rest = own[2, band] + from_inner[1, band].astype(f32)
+                final[band] = rest.astype(jnp.bfloat16)
+                rest_ahead(at).start()
+
+        @pl.when(jnp.logical_not(ahead_too))
+        def _():
+            for at in range(bands):
+                to_inner(2, at).wait_recv()
+                over_middle(1, at).wait_recv()
+                finish(at, [own.at[2], from_outer.at[2], from_inner.at[1]])
+
         for at in range(bands):
             over_middle(0, at).wait_send()
             over_middle(1, at).wait_send()
             to_end(at).wait_send()
-
-    for group in range(groups):
-        send_kv(0, 2, group, partner, 0).wait_send()
-        send_kv(0, 1, group, partner, 1).wait_send()
-        send_kv(2, 1, group, partner, 2).wait_send()
-    for at in range(bands):
-        hand(at).wait()
+        for at in range(bands):
+            hand(at).wait_send()
+
+        @pl.when(from_last)
+        def _():
+            for at in range(bands):
+                rest_ahead(at).wait_recv()
+                skip_ahead(at).wait_recv()
+                band = slice(at * piece, (at + 1) * piece)
+                total = from_behind[at].astype(f32) + from_mate[at].astype(f32)
+                out_ref[0, band] = total.astype(jnp.bfloat16)
+
+        @pl.when(jnp.logical_not(from_last))
+        def _():
+            for at in range(bands):
+                hand(at).wait_recv()
+
+    for part_at in range(2 * groups):
+        send_kv(0, 2, part_at, partner, 0).wait_send()
+        send_kv(0, 1, part_at, partner, 1).wait_send()
+        send_kv(2, 1, part_at, partner, 2).wait_send()
 
 
 def solution(mesh):
@@ -344,21 +430,25 @@
                 pltpu.VMEM(query_weight.shape[1:], bf16),
                 pltpu.VMEM(output_weight.shape[1:], bf16),
                 pltpu.VMEM((rows, width), bf16),
-                pltpu.VMEM((4, groups, rows, 2 * HD), bf16),
+                pltpu.VMEM((4, 2 * groups, rows, HD), bf16),
                 pltpu.VMEM((heads, rows, HD), bf16),
+                pltpu.VMEM((heads, 4, rows, HD), bf16),
                 pltpu.VMEM((rows, heads * HD), bf16),
                 pltpu.VMEM((4, rows, HD), jnp.float32),
                 pltpu.VMEM((4, rows, cols), jnp.float32),
                 pltpu.VMEM((3, rows, cols), bf16),
                 pltpu.VMEM((3, rows, cols), bf16),
                 pltpu.VMEM((2, rows, cols), bf16),
+                pltpu.VMEM((bands, PIECE, cols), bf16),
+                pltpu.VMEM((bands, PIECE, cols), bf16),
                 pltpu.VMEM((rows, cols), bf16),
                 pltpu.SemaphoreType.DMA((5 + DEPTHS,)),
-                pltpu.SemaphoreType.DMA((3, groups)),
-                pltpu.SemaphoreType.DMA((4, groups)),
+                pltpu.SemaphoreType.DMA((3, 2 * groups)),
+                pltpu.SemaphoreType.DMA((4, 2 * groups)),
                 pltpu.SemaphoreType.DMA((3, bands)),
                 pltpu.SemaphoreType.DMA((3, bands)),
                 pltpu.SemaphoreType.DMA((2, bands)),
+                pltpu.SemaphoreType.DMA((bands,)),
                 pltpu.SemaphoreType.DMA((bands,)),
                 pltpu.SemaphoreType.DMA((bands,)),
             ],

time: 57.7 us -> 55.8 us (0.967)
  the two profiles are of different devices: /device:TPU:8 before, /device:TPU:16 now
where the time goes in v4:
time: 55.8 us; the launch traced here: 55.7 us
  Pallas kernels  54.3 us (97%)
  local copies, waits for them, and re-layouts  0.71 us (1%)
  between operations  0.66 us (1%)
    pallas_call x1, Pallas kernels, body(): pl.pallas_call(functools.partial(block_kernel, n_seg, n_ctx, n_tp, PIECE)...  54.3 us

profile of v4, /device:TPU:16, one launch (start us, length us, event | category | flops | bytes accessed | tf_op | source)
XLA Modules:
  0.0 55.7 jit_solution(8959970771766249765)
XLA Ops:
  0.7 54.3 %shard_map.73 = bf16[1,128,1024]{2,1,0:T(8,128)(2,1)S(1)} custom-call(s32[1]{0:T(128)S(6)} %copy.10.win_ref, bf16[1,4096]{1,0:T(2,128)(2,1)} %gain_hbm.1, f32[1,128]{1,0:T(1,128)} %constant.2.clone.inv_hbm, bf16[1,128,4096]{2,1,0:T(8,128)(2,1)} %hid_hbm.1, bf16[1,4096,512]{2,1,0:T(8,128)(2,1)} %wkv_hbm.1, bf16[1,4096,1024]{2,1,0:T(8,128)(2,1)} %wq_hbm.1, ...), custom_call_target="tpu_custom_call" | custom-call | tf_op jit(solution)/shard_map/pallas_call | solution.py:420
  55.0 0.7 %copy.9 = bf16[1,128,1024]{2,1,0:T(8,128)(2,1)} copy(bf16[1,128,1024]{2,1,0:T(8,128)(2,1)S(1)} %shard_map.73) | data formatting | bytes 524288

commit v5 on v4

--- a/solution.py
+++ b/solution.py
@@ -95,15 +95,10 @@
     at_end = lax.rem(tp, 3) == 0
 
     barrier = pltpu.get_barrier_semaphore()
-    peers = [partner]
-    peers += [at_ctx(steps) for steps in (2, -2, 3, -3)]
-    peers += [{"tp": lax.rem(tp + step, n_tp)} for step in range(1, n_tp)]
-    peers += [
-        {"segment": lax.rem(seg + 1, n_seg)},
-        {"segment": lax.rem(seg + n_seg - 1, n_seg)},
-        {"segment": lax.rem(seg + 1, n_seg), "tp": mate},
-        {"segment": lax.rem(seg + n_seg - 1, n_seg), "tp": mate},
-    ]
+    behind = lax.rem(seg + n_seg - 1, n_seg)
+    peers = [partner, at_ctx(-2), at_ctx(-3)]
+    peers += [{"tp": mate}, {"tp": n_tp - 1 - tp}]
+    peers += [{"segment": behind}, {"segment": behind, "tp": mate}]
     for peer in peers:
         pl.semaphore_signal(barrier, inc=1, device_id=peer, device_id_type=MESH)
 
@@ -352,12 +347,12 @@
             add_on(0, at, own.at[0], from_outer.at[0])
             over_middle(0, at).start()
         for at in range(bands):
+            over_middle(0, at).wait_recv()
+            add_on(2, at, own.at[3], from_inner.at[0])
+            to_end(at).start()
             to_inner(1, at).wait_recv()
             add_on(1, at, own.at[1], from_outer.at[1])
             over_middle(1, at).start()
-            over_middle(0, at).wait_recv()
-            add_on(2, at, own.at[3], from_inner.at[0])
-            to_end(at).start()
 
         @pl.when(ahead_too)
         def _():

time: 55.8 us -> 54.4 us (0.975)
  the two profiles are of different devices: /device:TPU:16 before, /device:TPU:8 now
where the time goes in v5:
time: 54.4 us; the launch traced here: 54.3 us
  Pallas kernels  52.9 us (97%)
  local copies, waits for them, and re-layouts  0.71 us (1%)
  between operations  0.66 us (1%)
    pallas_call x1, Pallas kernels, body(): pl.pallas_call(functools.partial(block_kernel, n_seg, n_ctx, n_tp, PIECE)...  52.9 us

profile of v5, /device:TPU:8, one launch (start us, length us, event | category | flops | bytes accessed | tf_op | source)
XLA Modules:
  0.0 54.3 jit_solution(3318933739097986125)
XLA Ops:
  0.7 52.9 %shard_map.73 = bf16[1,128,1024]{2,1,0:T(8,128)(2,1)S(1)} custom-call(s32[1]{0:T(128)S(6)} %copy.10.win_ref, bf16[1,4096]{1,0:T(2,128)(2,1)} %gain_hbm.1, f32[1,128]{1,0:T(1,128)} %constant.2.clone.inv_hbm, bf16[1,128,4096]{2,1,0:T(8,128)(2,1)} %hid_hbm.1, bf16[1,4096,512]{2,1,0:T(8,128)(2,1)} %wkv_hbm.1, bf16[1,4096,1024]{2,1,0:T(8,128)(2,1)} %wq_hbm.1, ...), custom_call_target="tpu_custom_call" | custom-call | tf_op jit(solution)/shard_map/pallas_call | solution.py:415
  53.6 0.7 %copy.9 = bf16[1,128,1024]{2,1,0:T(8,128)(2,1)} copy(bf16[1,128,1024]{2,1,0:T(8,128)(2,1)S(1)} %shard_map.73) | data formatting | bytes 524288

commit v6 on v5

--- a/solution.py
+++ b/solution.py
@@ -11,6 +11,7 @@
 HD = 128
 PIECE = 16
 DEPTHS = 4
+FAR = 3
 NORM_EPS = 1e-05
 MESH = pl.DeviceIdType.MESH
 LOG2E = 1.4426950408889634
@@ -45,6 +46,7 @@
     part,
     from_outer,
     from_inner,
+    from_far,
     from_mate,
     from_behind,
     final,
@@ -54,6 +56,7 @@
     rs_send,
     outer_recv,
     inner_recv,
+    far_recv,
     mate_recv,
     z_send,
     z_recv,
@@ -98,7 +101,8 @@
     behind = lax.rem(seg + n_seg - 1, n_seg)
     peers = [partner, at_ctx(-2), at_ctx(-3)]
     peers += [{"tp": mate}, {"tp": n_tp - 1 - tp}]
-    peers += [{"segment": behind}, {"segment": behind, "tp": mate}]
+    across_two = lax.rem(tp + 2, n_tp)
+    peers += [{"segment": behind, "tp": other} for other in (tp, mate, across_two)]
     for peer in peers:
         pl.semaphore_signal(barrier, inc=1, device_id=peer, device_id_type=MESH)
 
@@ -236,6 +240,7 @@
     load_wo.wait()
 
     bands = rows // piece
+    near = bands - FAR
     ahead_too = seg == n_seg - 1
     from_last = seg == 0
 
@@ -270,6 +275,16 @@
             device_id_type=MESH,
         )
 
+    def skip_far(at):
+        return pltpu.make_async_remote_copy(
+            src_ref=part.at[1, pl.ds(at * piece, piece)],
+            dst_ref=from_far.at[at - near],
+            send_sem=rs_send.at[1, at],
+            recv_sem=far_recv.at[at - near],
+            device_id={"segment": lax.rem(seg + 1, n_seg), "tp": across_two},
+            device_id_type=MESH,
+        )
+
     def rest_ahead(at):
         return pltpu.make_async_remote_copy(
             src_ref=final.at[pl.ds(at * piece, piece)],
@@ -302,20 +317,20 @@
             @pl.when(at_end)
             def _():
                 part[step] = share.astype(jnp.bfloat16)
-                if step < 2:
-                    for at in range(bands):
-                        to_inner(step, at).start()
-                else:
+                direct = (bands, near, 0)[step]
+                for at in range(direct):
+                    to_inner(step, at).start()
+                if direct < bands:
 
                     @pl.when(ahead_too)
                     def _():
-                        for at in range(bands):
-                            skip_ahead(at).start()
+                        for at in range(direct, bands):
+                            (skip_far if step == 1 else skip_ahead)(at).start()
 
                     @pl.when(jnp.logical_not(ahead_too))
                     def _():
-                        for at in range(bands):
-                            to_inner(2, at).start()
+                        for at in range(direct, bands):
+                            to_inner(step, at).start()
 
     def finish(at, terms):
         band = slice(at * piece, (at + 1) * piece)
@@ -350,9 +365,23 @@
             over_middle(0, at).wait_recv()
             add_on(2, at, own.at[3], from_inner.at[0])
             to_end(at).start()
-            to_inner(1, at).wait_recv()
-            add_on(1, at, own.at[1], from_outer.at[1])
-            over_middle(1, at).start()
+            if at < near:
+                to_inner(1, at).wait_recv()
+                add_on(1, at, own.at[1], from_outer.at[1])
+                over_middle(1, at).start()
+            else:
+
+                @pl.when(ahead_too)
+                def _():
+                    band = slice(at * piece, (at + 1) * piece)
+                    part[1, band] = own[1, band].astype(jnp.bfloat16)
+                    over_middle(1, at).start()
+
+                @pl.when(jnp.logical_not(ahead_too))
+                def _():
+                    to_inner(1, at).wait_recv()
+                    add_on(1, at, own.at[1], from_outer.at[1])
+                    over_middle(1, at).start()
 
         @pl.when(ahead_too)
         def _():
@@ -384,6 +413,9 @@
                 skip_ahead(at).wait_recv()
                 band = slice(at * piece, (at + 1) * piece)
                 total = from_behind[at].astype(f32) + from_mate[at].astype(f32)
+                if at >= near:
+                    skip_far(at).wait_recv()
+                    total = total + from_far[at - near].astype(f32)
                 out_ref[0, band] = total.astype(jnp.bfloat16)
 
         @pl.when(jnp.logical_not(from_last))
@@ -434,6 +466,7 @@
                 pltpu.VMEM((3, rows, cols), bf16),
                 pltpu.VMEM((3, rows, cols), bf16),
                 pltpu.VMEM((2, rows, cols), bf16),
+                pltpu.VMEM((FAR, PIECE, cols), bf16),
                 pltpu.VMEM((bands, PIECE, cols), bf16),
                 pltpu.VMEM((bands, PIECE, cols), bf16),
                 pltpu.VMEM((rows, cols), bf16),
@@ -443,6 +476,7 @@
                 pltpu.SemaphoreType.DMA((3, bands)),
                 pltpu.SemaphoreType.DMA((3, bands)),
                 pltpu.SemaphoreType.DMA((2, bands)),
+                pltpu.SemaphoreType.DMA((FAR,)),
                 pltpu.SemaphoreType.DMA((bands,)),
                 pltpu.SemaphoreType.DMA((bands,)),
                 pltpu.SemaphoreType.DMA((bands,)),

time: 54.4 us -> 53.7 us (0.987)
  Pallas kernels: 52.9 us -> 52.2 us
    pallas_call x1, Pallas kernels: 52.9 us -> 52.2 us  [body(): pl.pallas_call(functools.partial(block_kernel, n_seg, n_ctx, n_tp, PIECE)...]
where the time goes in v6:
time: 53.7 us; the launch traced here: 53.5 us
  Pallas kernels  52.2 us (97%)
  local copies, waits for them, and re-layouts  0.71 us (1%)
  between operations  0.66 us (1%)
    pallas_call x1, Pallas kernels, body(): pl.pallas_call(functools.partial(block_kernel, n_seg, n_ctx, n_tp, PIECE)...  52.2 us

profile of v6, /device:TPU:8, one launch (start us, length us, event | category | flops | bytes accessed | tf_op | source)
XLA Modules:
  0.0 53.5 jit_solution(16427492163282346667)
XLA Ops:
  0.7 52.2 %shard_map.73 = bf16[1,128,1024]{2,1,0:T(8,128)(2,1)S(1)} custom-call(s32[1]{0:T(128)S(6)} %copy.10.win_ref, bf16[1,4096]{1,0:T(2,128)(2,1)} %gain_hbm.1, f32[1,128]{1,0:T(1,128)} %constant.2.clone.inv_hbm, bf16[1,128,4096]{2,1,0:T(8,128)(2,1)} %hid_hbm.1, bf16[1,4096,512]{2,1,0:T(8,128)(2,1)} %wkv_hbm.1, bf16[1,4096,1024]{2,1,0:T(8,128)(2,1)} %wq_hbm.1, ...), custom_call_target="tpu_custom_call" | custom-call | tf_op jit(solution)/shard_map/pallas_call | solution.py:447
  52.8 0.7 %copy.9 = bf16[1,128,1024]{2,1,0:T(8,128)(2,1)} copy(bf16[1,128,1024]{2,1,0:T(8,128)(2,1)S(1)} %shard_map.73) | data formatting | bytes 524288
